TPU v7x, 32 devices: a whole 2x2x4 slice. The times are simulated.
32 devices in a mesh: lon: 8 (over z, x), lat: 4 (over y, core).
Axes of the slice: x: 2, y: 2, z: 4, core: 2. Of those that a mesh axis runs over, the one named last changes fastest.
Arguments:
- grid_field: float32 [4, 64, 16, 2048], P(None, 'lat', None, 'lon'), may hold values from -6 to 6
- lat_weight: float32 [64], replicated, may hold values from 0.3 to 3
Outputs:
- spec_real: float32 [4, 64, 16, 1024], P(None, None, 'lat', 'lon')
- spec_imag: float32 [4, 64, 16, 1024], P(None, None, 'lat', 'lon')
All inputs are finite; a program needn't handle non-finite values.
Results may differ from a plain program's by a relative error of at most 0.000071.
Values sent between devices are 32-bit elements; how exact they have to be, the bound alone decides.
A program may use at most 64 MiB of HBM per device.

v0:
```python
import math
import jax
import jax.numpy as jnp
from jax import lax
from jax.sharding import PartitionSpec as P

MODES = 1024
two_pi = 2.0 * math.pi


def mode_table(lon_ids, mode_ids, length):
    phases = lon_ids[:, None] * mode_ids[None, :] % length
    angles = phases.astype(jnp.float32) * (two_pi / length)
    normalizer = 1.0 / math.sqrt(length)
    return (jnp.cos(angles) * normalizer, -jnp.sin(angles) * normalizer)


def per_device(grid_field, lat_weight):
    fields, lat_dev, radius_count, lon_dev = grid_field.shape
    cycle_size = lax.axis_size("lon")
    length = cycle_size * lon_dev
    mode_dev = MODES // cycle_size
    my_index = lax.axis_index("lon")
    row_count = fields * lat_dev * radius_count
    flat_grid = grid_field.reshape(row_count, lon_dev)
    mode_ids = my_index * mode_dev + jnp.arange(mode_dev, dtype=jnp.int32)
    lon_block = lax.all_gather(flat_grid, "lon", axis=1, tiled=True)
    lon_ids = jnp.arange(lon_block.shape[1], dtype=jnp.int32)
    cosine, sine_part = mode_table(lon_ids, mode_ids, length)
    dft_table = jnp.concatenate([cosine, sine_part], axis=1)
    summed = jnp.dot(
        lon_block, dft_table, precision=lax.Precision.HIGHEST, preferred_element_type=jnp.float32
    )
    spectra = summed.reshape(fields, lat_dev, radius_count, 2, mode_dev)
    gathered = lax.all_to_all(spectra, "lat", split_axis=2, concat_axis=1, tiled=True)
    weights_row = lat_weight[None, :, None, None]
    return (gathered[:, :, :, 0, :] * weights_row, gathered[:, :, :, 1, :] * weights_row)


def solution(mesh):
    in_specs = (P(None, "lat", None, "lon"), P())
    out_specs = (P(None, None, "lat", "lon"), P(None, None, "lat", "lon"))
    return jax.shard_map(
        per_device, mesh=mesh, in_specs=in_specs, out_specs=out_specs, check_vma=False
    )
```

profile of v0, /device:TPU:0, one launch (start us, length us, event | category | flops | bytes accessed | tf_op | source)
XLA Modules:
  0.0 181.7 jit_solution(17533059803057809148)
XLA Ops:
  7.2 0.0 all-gather.2.cloned.1.call-start
  7.2 0.7 all-gather.2.cloned.1.call-update
  7.9 4.2 %cosine_multiply_fusion = (f32[2048,128]{1,0:T(8,128)S(1)}, f32[2048,128]{1,0:T(8,128)S(1)}) fusion(s32[128]{0:T(128)S(1)} %iota_add_fusion), kind=kLoop, calls=%fused_computation.12 | loop fusion | flops 4456448 | bytes 2097664 | tf_op jit(solution)/shard_map/mul | solution.py:15
  12.1 125.6 %all-gather.2.cloned.1.call-done = f32[1024,2048]{1,0:T(8,128)} async-done(((f32[1024,256]{1,0:T(8,128)}), f32[1024,2048]{1,0:T(8,128)}) %all-gather.2.cloned.1.call-update) | async-done | bytes 8388624 | tf_op jit(solution)/shard_map/all_gather | solution.py:27
  137.7 15.9 %fusion.4 = f32[1024,256]{0,1:T(8,128)S(1)} fusion(f32[1024,2048]{1,0:T(8,128)} %all-gather.2.cloned.1.call-done, f32[2048,128]{1,0:T(8,128)S(1)} %get-tuple-element.9, f32[2048,128]{1,0:T(8,128)S(1)} %get-tuple-element.8), kind=kOutput, calls=%fused_computation.7 | convolution fusion | flops 6442975232 | bytes 11534336 | tf_op jit(solution)/shard_map/dot_general | solution.py:31
  153.6 0.0 copy-start
  153.6 0.3 copy.13
  154.0 0.5 reshape.16
  154.5 0.6 copy.14
  155.1 17.0 %all_to_all.18 = f32[4,16,16,2,128]{4,3,1,0,2:T(2,128)S(1)} all-to-all(f32[4,16,16,2,128]{4,3,1,0,2:T(2,128)S(1)} %copy.14), channel_id=1, replica_groups=mesh['lon'=8,'lat'=4] {'lat'}, dimensions={2} | all-to-all | bytes 2097152 | tf_op jit(solution)/shard_map/all_to_all | solution.py:35
  172.1 0.1 copy.15
  172.2 0.1 copy.16
  172.4 0.0 copy-done
  172.4 0.2 fusion.13
  172.6 1.1 copy.19
  173.7 1.1 copy.18
  (1 shorter events, 0.0 us)
Async XLA Ops:
  7.2 130.5 %all-gather.2.cloned.1.call-start = ((), (), s32[]{:S(2)}) async-start(), calls=%async_computation.1 | async-start | bytes 9437184 | tf_op jit(solution)/shard_map/all_gather | solution.py:27
  153.6 18.8 %copy-start = (f32[64]{0:T(128)S(1)}, f32[64]{0:T(128)}, u32[]{:S(2)}) copy-start(f32[64]{0:T(128)} %param.3) | copy-start | bytes 772
Sparse Core Ops, SparseCore 0:
  10.0 127.6 all-gather.1
where the time goes:
time: 182 us
  waiting for transfers between devices  126 us (69%)
  blocking collectives  17 us (9%)
  matrix products  15.9 us (9%)
  between operations  14.1 us (8%)
  other arithmetic  4.36 us (2%)
  local copies, waits for them, and re-layouts  3.95 us (2%)
    all_gather x1, waiting for transfers between devices, per_device(): lon_block = lax.all_gather(flat_grid, 'lon', axis=1, tiled=True)  126 us
    all_to_all x1, blocking collectives, per_device(): lax.all_to_all(spectra, 'lat', split_axis=2, concat_axis=1, tiled=True)  17 us
    dot_general x1, matrix products, per_device(): jnp.dot(lon_block, dft_table, precision=lax.Precision.HIGHEST, preferred_...  15.9 us
    mul x1, other arithmetic, mode_table(): return (jnp.cos(angles) * normalizer, -jnp.sin(angles) * normalizer)  4.17 us
  transfers between devices with their start and end apart: 1, of which 1 were waited for; matrix products, arithmetic and copies ran while one was open for 2% of the time, Pallas kernels for 0%

commit v1 on v0

--- a/solution.py
+++ b/solution.py
@@ -24,7 +24,10 @@
     row_count = fields * lat_dev * radius_count
     flat_grid = grid_field.reshape(row_count, lon_dev)
     mode_ids = my_index * mode_dev + jnp.arange(mode_dev, dtype=jnp.int32)
-    lon_block = lax.all_gather(flat_grid, "lon", axis=1, tiled=True)
+    lon_block = jnp.concatenate(
+        lax.all_to_all(jnp.stack([flat_grid for _ in range(lax.axis_size("lon"))]), "lon", 0, 0),
+        axis=1,
+    )
     lon_ids = jnp.arange(lon_block.shape[1], dtype=jnp.int32)
     cosine, sine_part = mode_table(lon_ids, mode_ids, length)
     dft_table = jnp.concatenate([cosine, sine_part], axis=1)

time: 182 us -> 228 us (1.25)
  waiting for transfers between devices: 126 us -> 179 us
  between operations: 14.1 us -> 0.72 us
  starting transfers between devices: 0.04 us -> 7.28 us
  matrix products: 15.9 us -> 9.61 us
  local copies, waits for them, and re-layouts: 3.95 us -> 9.78 us
    all_to_all x0 -> x1, waiting for transfers between devices: none -> 179 us  [per_device(): lax.all_to_all(jnp.stack([flat_grid for _ in range(lax.axis_size('lon'))]...]
    all_gather x1 -> x0, waiting for transfers between devices: 126 us -> none  [per_device(): lon_block = lax.all_gather(flat_grid, 'lon', axis=1, tiled=True)]
    all_to_all x0 -> x1, starting transfers between devices: none -> 7.28 us  [per_device(): lax.all_to_all(jnp.stack([flat_grid for _ in range(lax.axis_size('lon'))]...]
    dot_general x1, matrix products: 15.9 us -> 9.61 us  [per_device(): jnp.dot(lon_block, dft_table, precision=lax.Precision.HIGHEST, preferred_...]
    another operation x0 -> x2, local copies, waits for them, and re-layouts: none -> 5.84 us  [per_device(): jnp.stack([flat_grid for _ in range(lax.axis_size('lon'))])]
where the time goes in v1:
time: 228 us
  waiting for transfers between devices  179 us (79%)
  blocking collectives  17 us (7%)
  local copies, waits for them, and re-layouts  9.78 us (4%)
  matrix products  9.61 us (4%)
  starting transfers between devices  7.28 us (3%)
  other arithmetic  4.36 us (2%)
    all_to_all x1, waiting for transfers between devices, per_device(): lax.all_to_all(jnp.stack([flat_grid for _ in range(lax.axis_size('lon'))]...  179 us
    all_to_all x1, blocking collectives, per_device(): lax.all_to_all(spectra, 'lat', split_axis=2, concat_axis=1, tiled=True)  17 us
    dot_general x1, matrix products, per_device(): jnp.dot(lon_block, dft_table, precision=lax.Precision.HIGHEST, preferred_...  9.61 us
    all_to_all x1, starting transfers between devices, per_device(): lax.all_to_all(jnp.stack([flat_grid for _ in range(lax.axis_size('lon'))]...  7.28 us
    another operation x2, local copies, waits for them, and re-layouts, per_device(): jnp.stack([flat_grid for _ in range(lax.axis_size('lon'))])  5.84 us
  transfers between devices with their start and end apart: 1, of which 1 were waited for; matrix products, arithmetic and copies ran while one was open for 2% of the time, Pallas kernels for 0%

profile of v1, /device:TPU:0, one launch (start us, length us, event | category | flops | bytes accessed | tf_op | source)
XLA Modules:
  0.0 227.8 jit_solution(13551627884268721358)
XLA Ops:
  0.6 1.6 copy.15
  2.2 4.3 %stack.3 = f32[8,1024,256]{1,2,0:T(8,128)} broadcast(f32[1024,256]{0,1:T(8,128)S(1)} %copy.15), dimensions={1,2} | broadcast | bytes 9437184 | tf_op jit(solution)/shard_map/stack | solution.py:28
  6.5 7.3 %all-to-all-start = ((f32[8,1024,256]{1,2,0:T(8,128)}), f32[8,1024,256]{1,2,0:T(8,128)}, u32[]{:S(2)}, u32[]{:S(2)}) async-start(f32[8,1024,256]{1,2,0:T(8,128)} %stack.3), calls=%async_computation | async-start | bytes 16777216 | tf_op jit(solution)/shard_map/all_to_all | solution.py:28
  13.8 4.2 %cosine_multiply_fusion = (f32[2048,128]{1,0:T(8,128)S(1)}, f32[2048,128]{1,0:T(8,128)S(1)}) fusion(s32[128]{0:T(128)S(1)} %iota_add_fusion), kind=kLoop, calls=%fused_computation.12 | loop fusion | flops 4456448 | bytes 2097664 | tf_op jit(solution)/shard_map/mul | solution.py:15
  17.9 179.0 %all-to-all-done = f32[8,1024,256]{1,2,0:T(8,128)} async-done(((f32[8,1024,256]{1,2,0:T(8,128)}), f32[8,1024,256]{1,2,0:T(8,128)}, u32[]{:S(2)}, u32[]{:S(2)}) %all-to-all-start) | async-done | bytes 8388640 | tf_op jit(solution)/shard_map/all_to_all | solution.py:28
  196.9 9.6 %fusion.4 = f32[1024,256]{0,1:T(8,128)S(1)} fusion(f32[1024,2048]{0,1:T(8,128)} %bitcast.2, f32[2048,128]{1,0:T(8,128)S(1)} %get-tuple-element.9, f32[2048,128]{1,0:T(8,128)S(1)} %get-tuple-element.8), kind=kOutput, calls=%fused_computation.7 | convolution fusion | flops 6442975232 | bytes 11534336 | tf_op jit(solution)/shard_map/dot_general | solution.py:34
  206.5 0.0 copy-start
  206.6 0.3 copy.16
  206.9 0.5 reshape.22
  207.4 0.6 copy.17
  208.0 17.0 %all_to_all.23 = f32[4,16,16,2,128]{4,3,1,0,2:T(2,128)S(1)} all-to-all(f32[4,16,16,2,128]{4,3,1,0,2:T(2,128)S(1)} %copy.17), channel_id=1, replica_groups=mesh['lon'=8,'lat'=4] {'lat'}, dimensions={2} | all-to-all | bytes 2097152 | tf_op jit(solution)/shard_map/all_to_all | solution.py:38
  225.1 0.1 copy.18
  225.1 0.1 copy.19
  225.3 0.0 copy-done
  225.3 0.2 fusion.13
  225.5 1.1 copy.21
  226.6 1.1 copy.22
  (1 shorter events, 0.0 us)
Async XLA Ops:
  6.5 190.4 %all-to-all-start = ((f32[8,1024,256]{1,2,0:T(8,128)}), f32[8,1024,256]{1,2,0:T(8,128)}, u32[]{:S(2)}, u32[]{:S(2)}) async-start(f32[8,1024,256]{1,2,0:T(8,128)} %stack.3), calls=%async_computation | async-start | bytes 16777216 | tf_op jit(solution)/shard_map/all_to_all | solution.py:28
  206.5 18.7 %copy-start = (f32[64]{0:T(128)S(1)}, f32[64]{0:T(128)}, u32[]{:S(2)}) copy-start(f32[64]{0:T(128)} %param.3) | copy-start | bytes 772
